TPU v7x, 128 devices: a whole 4x4x4 slice. The times are simulated.
128 devices in a mesh: row: 8 (over z_lo, y), col: 16 (over z_hi, x, core).
Axes of the slice: x: 4, y: 4, z: 4 (z_hi: 2, z_lo: 2; z = z_hi * 2 + z_lo), core: 2. Of those that a mesh axis runs over, the one named last changes fastest.
Arguments:
- slip: float32 [262144, 256], P(('row', 'col')), may hold values from -2 to 2
- state: float32 [262144, 256], P(('row', 'col')), may hold values from 0.4 to 0.9
- tau_load: float32 [262144], P(('row', 'col')), may hold values from 1 to 2
- normal_stress: float32 [262144], P(('row', 'col')), may hold values from 6 to 8
- direct_effect: float32 [262144], P(('row', 'col')), may hold values from 0.8 to 1.6
- evolution_effect: float32 [262144], P(('row', 'col')), may hold values from 0.5 to 1
- slip_distance: float32 [262144], P(('row', 'col')), may hold values from 0.5 to 2
- self_stiffness: float32 [262144], P(('row', 'col')), may hold values from 0.5 to 2
- near_blocks: bfloat16 [3, 262144, 256], P(None, ('row', 'col')), may hold values from -0.21875 to 0.21875
- basis_in: bfloat16 [32, 262144], P(None, ('row', 'col')), may hold values from -0.375 to 0.375
- basis_out: bfloat16 [32, 262144], P(None, ('row', 'col')), may hold values from -1 to 1
- coupling: bfloat16 [32768, 8, 4096], P('row', None, 'col'), may hold values from -0.046875 to 0.046875
- block_rank: int32 [1024, 8, 128], P('row', None, 'col'), may hold values from 8 to 32
- adj_bricks: int32 [8, 262144], P(None, ('row', 'col')), may hold values from 0 to 2047
- adj_count: int32 [262144], P(('row', 'col')), may hold values from 1 to 8
- adj_weight: float32 [8, 262144], P(None, ('row', 'col')), may hold values from 0.05 to 1
- pressure_now: bfloat16 [2048, 256], P('col'), may hold values from 0.099609375 to 1
- pressure_rate: bfloat16 [2048, 256], P('col'), may hold values from 0.5 to 5
Outputs:
- slip_out: float32 [262144, 256], P(('row', 'col'))
- state_out: float32 [262144, 256], P(('row', 'col'))
Inputs may be any that keep to these rules, and one draw needn't show every extreme that they name: Only the first adj_count entries of a patch's brick list are read. `adj_bricks`: brick numbers index the whole reservoir. `block_rank`: ranks of pairs with |i - j| <= 1 are not read.
All inputs are finite; a program needn't handle non-finite values.
Results may differ from a plain program's by a relative error of at most 0.0007.
Values may be sent and summed in bfloat16 or wider, within the bound.
A program may use at most 192 MiB of HBM per device.

v0:
```python
import jax
import jax.numpy as jnp
from jax import lax
from jax.sharding import PartitionSpec as P

BS = 256
R = 32
BPD = 8
STEP_SIZE = 0.5
REF_FRICTION = 0.6


def with_halo(array, sides, width):
    for axis, dim in sides:
        devices, length = (lax.axis_size(axis), array.shape[dim])
        up = [(i, (i + 1) % devices) for i in range(devices - 1)]
        down = [(j, i) for i, j in up]
        last = lax.slice_in_dim(array, length - width, length, axis=dim)
        initial = lax.slice_in_dim(array, 0, width, axis=dim)
        before = lax.ppermute(last, axis, up)
        after = lax.ppermute(initial, axis, down)
        array = jnp.concatenate([before, array, after], axis=dim)
    return array


def fault_pressure(joined, adj_bricks, adj_count, adj_weight):
    slots = adj_bricks.shape[0]
    patches = adj_bricks.shape[1]
    slot_ids = jnp.arange(slots, dtype=jnp.int32)
    live = (adj_count[None, :] > slot_ids[:, None]).astype(jnp.float32)
    weighting = adj_weight * live
    weight_sum = jnp.sum(weighting, axis=0)
    picked = joined[adj_bricks.reshape(slots * patches)].reshape(slots, patches, joined.shape[1])
    total = jnp.sum(weighting[:, :, None] * picked.astype(jnp.float32), axis=0)
    return total / weight_sum[:, None]


def far_mask_flat(row_blocks, col_blocks, ranks):
    row_total = row_blocks.shape[0]
    col_total = col_blocks.shape[0]
    row_block_of = jnp.repeat(row_blocks, R)
    col_block_of = jnp.repeat(col_blocks, R)
    row_level = jnp.arange(row_total * R, dtype=jnp.int32) % R
    col_level = jnp.arange(col_total * R, dtype=jnp.int32) % R
    spread = (
        jnp.arange(col_total, dtype=jnp.int32)[:, None]
        == (jnp.arange(col_total * R, dtype=jnp.int32) // R)[None, :]
    ).astype(jnp.float32)
    rank_cols = jnp.dot(
        ranks.astype(jnp.float32),
        spread,
        precision=lax.Precision.HIGHEST,
        preferred_element_type=jnp.float32,
    )
    rank_full = jnp.broadcast_to(rank_cols[:, None, :], (row_total, R, col_total * R)).reshape(
        row_total * R, col_total * R
    )
    level = jnp.maximum(row_level[:, None], col_level[None, :]).astype(jnp.float32)
    apart = jnp.abs(row_block_of[:, None] - col_block_of[None, :]) > 1
    return apart & (level < rank_full)


def rates(
    slip_now,
    state_now,
    outer,
    pressure,
    tau_load,
    normal_stress,
    direct_effect,
    evolution_effect,
    slip_distance,
    self_stiffness,
):
    tau = tau_load[:, None] - self_stiffness[:, None] * slip_now - outer
    sigma = normal_stress[:, None] - pressure
    speed = jnp.exp((tau / sigma - state_now) / direct_effect[:, None])
    drift = (evolution_effect / slip_distance)[:, None] * (
        jnp.exp((REF_FRICTION - state_now) / evolution_effect[:, None]) - speed
    )
    return (speed, drift)


def project(basis, slips):
    count = slips.shape[0] // BS
    coeff = jnp.einsum(
        "rnb,nbe->nre",
        basis.reshape(R, count, BS),
        slips.reshape(count, BS, slips.shape[1]),
        preferred_element_type=jnp.float32,
    )
    return coeff.astype(jnp.bfloat16).reshape(count * R, slips.shape[1])


def near_field(padded, near_blocks):
    patches = near_blocks.shape[1]
    count = patches // BS
    terms = []
    for neighbour in range(3):
        window = padded[neighbour * BS : neighbour * BS + patches].reshape(
            count, BS, padded.shape[1]
        )
        terms.append(
            jnp.einsum(
                "gns,gsl->gnl",
                near_blocks[neighbour].reshape(count, BS, BS),
                window,
                preferred_element_type=jnp.float32,
            )
        )
    return (terms[0] + terms[1] + terms[2]).reshape(patches, padded.shape[1])


def per_device(
    slip,
    state,
    tau_load,
    normal_stress,
    direct_effect,
    evolution_effect,
    slip_distance,
    self_stiffness,
    near_blocks,
    basis_in,
    basis_out,
    coupling,
    block_rank,
    adj_bricks,
    adj_count,
    adj_weight,
    pressure_now,
    pressure_rate,
):
    now_all, rate_all = (
        lax.all_gather(pressure_now, "col", axis=0, tiled=True),
        lax.all_gather(pressure_rate, "col", axis=0, tiled=True),
    )
    scenarios = slip.shape[1]
    joined = jnp.concatenate([now_all, rate_all], 1)
    both_press = fault_pressure(joined, adj_bricks, adj_count, adj_weight)
    base_press = both_press[:, :scenarios]
    rate_press = both_press[:, scenarios:]
    row_count = lax.axis_size("row")
    col_count = lax.axis_size("col")
    row_index = lax.axis_index("row")
    col_index = lax.axis_index("col")
    matrix = coupling.reshape(coupling.shape[0], coupling.shape[1] * coupling.shape[2])
    ranks = block_rank.reshape(block_rank.shape[0], block_rank.shape[1] * block_rank.shape[2])
    row_blocks = row_index * (col_count * BPD) + jnp.arange(col_count * BPD, dtype=jnp.int32)
    source_rows = jnp.arange(row_count, dtype=jnp.int32)[:, None] * col_count + col_index
    col_blocks = (source_rows * BPD + jnp.arange(BPD, dtype=jnp.int32)[None, :]).reshape(
        row_count * BPD
    )
    keep = far_mask_flat(row_blocks, col_blocks, ranks)
    masked = jnp.where(keep, matrix, jnp.zeros((), jnp.bfloat16))
    share = BPD * R
    basis_all = lax.all_gather(basis_in, "row", axis=1, tiled=True)

    def stress(slip_now):
        rounded = slip_now.astype(jnp.bfloat16)
        slip_all = lax.all_gather(rounded, "row", axis=0, tiled=True)
        coeff = project(basis_all, slip_all)
        partial_sum = jnp.dot(masked, coeff, preferred_element_type=jnp.float32)
        total = lax.psum(partial_sum.astype(jnp.bfloat16), "col").astype(jnp.float32)
        mine = lax.dynamic_slice_in_dim(total, col_index * share, share, 0)
        far_coeff = mine.astype(jnp.bfloat16)
        far = jnp.einsum(
            "rnb,nre->nbe",
            basis_out.reshape(R, BPD, BS),
            far_coeff.reshape(BPD, R, slip_now.shape[1]),
            preferred_element_type=jnp.float32,
        )
        far = far.reshape(slip_now.shape)
        padded = with_halo(rounded, ((("row", "col"), 0),), BS)
        near = near_field(padded, near_blocks)
        return near + far

    params = (
        tau_load,
        normal_stress,
        direct_effect,
        evolution_effect,
        slip_distance,
        self_stiffness,
    )
    speed0, drift0 = rates(slip, state, stress(slip), base_press, *params)
    slip_mid = slip + STEP_SIZE * speed0
    state_mid = state + STEP_SIZE * drift0
    speed1, drift1 = rates(
        slip_mid, state_mid, stress(slip_mid), base_press + STEP_SIZE * rate_press, *params
    )
    slip_out = slip + 0.5 * STEP_SIZE * (speed0 + speed1)
    state_out = state + 0.5 * STEP_SIZE * (drift0 + drift1)
    return (slip_out, state_out)


def solution(mesh):
    in_specs = (
        P(("row", "col"), None),
        P(("row", "col"), None),
        P(("row", "col")),
        P(("row", "col")),
        P(("row", "col")),
        P(("row", "col")),
        P(("row", "col")),
        P(("row", "col")),
        P(None, ("row", "col"), None),
        P(None, ("row", "col")),
        P(None, ("row", "col")),
        P("row", None, "col"),
        P("row", None, "col"),
        P(None, ("row", "col")),
        P(("row", "col")),
        P(None, ("row", "col")),
        P("col", None),
        P("col", None),
    )
    out_specs = (P(("row", "col"), None), P(("row", "col"), None))
    return jax.shard_map(
        per_device, mesh=mesh, in_specs=in_specs, out_specs=out_specs, check_vma=False
    )
```

profile of v0, /device:TPU:1, one launch (start us, length us, event | category | flops | bytes accessed | tf_op | source)
XLA Modules:
  0.0 662.5 jit_solution(3476036359275173559)
XLA Ops:
  12.4 4.5 collective-permute-start
  20.7 11.4 %broadcast_in_dim.14 = f32[128,32,2048]{2,1,0:T(8,128)} broadcast(f32[128,2048]{1,0:T(8,128)S(1)} %copy.23), dimensions={0,2} | broadcast | bytes 34603008 | tf_op jit(solution)/shard_map/broadcast_in_dim | solution.py:55
  32.1 19.9 %copy.30 = f32[512,8,8,256]{3,2,1,0:T(8,128)S(1)} copy(f32[512,8,8,256]{3,1,2,0:T(8,128)} %bitcast.99) | data formatting | bytes 67108864
  52.1 22.4 %fusion.2 = bf16[4096,8,256]{2,1,0:T(8,128)(2,1)} fusion(bf16[4096,8,256]{2,1,0:T(8,128)(2,1)} %param.29, f32[512,8,8,256]{3,2,1,0:T(8,128)S(1)} %copy.30, s32[8,256]{1,0:T(8,128)S(1)} %add_select_fusion.2, s32[4096]{0:T(1024)S(1)} %add_select_fusion, s32[8,256]{1,0:T(8,128)S(1)} %broadcast_in_dim.13, s32[4096]{0:T(1024)S(1)} %sub.77), kind=kLoop, calls=%fused_computation.6 | loop fusion | flops 67108864 | bytes 67158016 | tf_op jit(solution)/shard_map/jit(_where)/select_n | solution.py:155
  74.5 16.5 %copy.31 = bf16[512,8,8,256]{3,1,2,0:T(8,128)(2,1)} copy(bf16[512,8,8,256]{3,2,1,0:T(8,128)(2,1)} %bitcast.101) | data formatting | bytes 33554432
  92.5 3.4 fusion.44
  99.9 45.0 %all-gather.8.cloned.1.call-done = bf16[16384,256]{1,0:T(8,128)(2,1)} async-done(((bf16[2048,256]{1,0:T(8,128)(2,1)}), bf16[16384,256]{1,0:T(8,128)(2,1)}) %all-gather.8.cloned.1.call-update) | async-done | bytes 8388624 | tf_op jit(solution)/shard_map/all_gather | solution.py:161
  144.8 5.2 convolution_convert_fusion.3
  150.0 9.6 %convolution_convert_fusion.1 = bf16[4096,256]{1,0:T(8,128)(2,1)} fusion(bf16[4096,2048]{1,0:T(8,128)(2,1)} %bitcast.106, bf16[2048,256]{1,0:T(8,128)(2,1)S(1)} %bitcast.121), kind=kOutput, calls=%fused_computation.8 | convolution fusion | flops 4296015872 | bytes 19922944 | tf_op jit(solution)/shard_map/dot_general | solution.py:163
  159.9 31.6 %all-gather.10.cloned.1.call-done = bf16[2048,256]{1,0:T(8,128)(2,1)} async-done(((bf16[128,256]{1,0:T(8,128)(2,1)}), bf16[2048,256]{1,0:T(8,128)(2,1)}) %all-gather.10.cloned.1.call-update) | async-done | bytes 1048592 | tf_op jit(solution)/shard_map/all_gather | solution.py:135
  191.5 45.9 %all-gather.12.cloned.1.call-done = bf16[2048,256]{1,0:T(8,128)(2,1)} async-done(((bf16[128,256]{1,0:T(8,128)(2,1)}), bf16[2048,256]{1,0:T(8,128)(2,1)}) %all-gather.12.cloned.1.call-update) | async-done | bytes 1048592 | tf_op jit(solution)/shard_map/all_gather | solution.py:136
  239.1 66.4 %gather_fusion = bf16[16384,512]{1,0:T(8,128)(2,1)} fusion(bf16[2048,512]{1,0:T(8,128)(2,1)S(1)} %pad_maximum_fusion, s32[16384]{0:T(1024)S(1)} %broadcast_clamp_fusion), kind=kCustom, calls=%fused_computation | custom fusion | bytes 33619968 | tf_op jit(solution)/shard_map/gather | solution.py:33
  305.5 7.5 %fusion = f32[2048,512]{1,0:T(8,128)S(1)} fusion(bf16[8,2048,512]{2,1,0:T(8,128)(2,1)} %bitcast.100, f32[8,2048]{1,0:T(8,128)S(1)} %get-tuple-element.7), kind=kLoop, calls=%fused_computation.3 | loop fusion | flops 24117248 | bytes 21037056 | tf_op jit(solution)/shard_map/reduce_sum | solution.py:34
  315.5 67.4 %all-reduce.3.cloned.1.call-done = bf16[4096,256]{1,0:T(8,128)(2,1)} async-done(((bf16[4096,256]{1,0:T(8,128)(2,1)}), bf16[4096,256]{1,0:T(8,128)(2,1)}) %all-reduce.3.cloned.1.call-update) | async-done | bytes 2097168 | tf_op jit(solution)/shard_map/psum | solution.py:164
  384.6 2.8 bitcast_add_fusion
  388.9 3.4 fusion.15
  392.4 93.1 %all-gather.14.cloned.1.call-done = bf16[16384,256]{1,0:T(8,128)(2,1)} async-done(((bf16[2048,256]{1,0:T(8,128)(2,1)}), bf16[16384,256]{1,0:T(8,128)(2,1)}) %all-gather.14.cloned.1.call-update) | async-done | bytes 8388624 | tf_op jit(solution)/shard_map/all_gather | solution.py:161
  485.5 4.8 convolution_convert_fusion.2
  490.3 9.7 %convolution_convert_fusion = bf16[4096,256]{1,0:T(8,128)(2,1)} fusion(bf16[4096,2048]{1,0:T(8,128)(2,1)} %bitcast.107, bf16[2048,256]{1,0:T(8,128)(2,1)S(1)} %bitcast.120), kind=kOutput, calls=%fused_computation.7 | convolution fusion | flops 4296015872 | bytes 19922944 | tf_op jit(solution)/shard_map/dot_general | solution.py:163
  501.2 3.8 collective-permute-start.2
  507.0 3.1 fusion.47
  515.5 127.8 %all-reduce.5.cloned.1.call-done = bf16[4096,256]{1,0:T(8,128)(2,1)} async-done(((bf16[4096,256]{1,0:T(8,128)(2,1)}), bf16[4096,256]{1,0:T(8,128)(2,1)}) %all-reduce.5.cloned.1.call-update) | async-done | bytes 2097168 | tf_op jit(solution)/shard_map/psum | solution.py:164
  644.9 2.9 add_add_fusion
  649.6 4.3 multiply_add_fusion
  (107 shorter events, 35.7 us)
Async XLA Ops:
  7.2 92.7 %all-gather.6.cloned.1.call-start = ((), (), s32[]{:S(2)}) async-start(), calls=%async_computation | async-start | bytes 1179648 | tf_op jit(solution)/shard_map/all_gather | solution.py:157
  7.9 11.5 %copy-start.24 = (s32[128,8,8]{0,2,1:T(8,128)S(1)}, s32[128,8,8]{0,2,1:T(8,128)}, u32[]{:S(2)}) copy-start(s32[128,8,8]{0,2,1:T(8,128)} %param.30) | copy-start | bytes 98308
  7.9 136.9 %all-gather.8.cloned.1.call-start = ((), (), s32[]{:S(2)}) async-start(), calls=%async_computation.1 | async-start | bytes 9437184 | tf_op jit(solution)/shard_map/all_gather | solution.py:161
  10.6 180.9 %all-gather.10.cloned.1.call-start = ((), (), s32[]{:S(2)}) async-start(), calls=%async_computation.3 | async-start | bytes 1114112 | tf_op jit(solution)/shard_map/all_gather | solution.py:135
  11.4 226.0 %all-gather.12.cloned.1.call-start = ((), (), s32[]{:S(2)}) async-start(), calls=%async_computation.4 | async-start | bytes 1114112 | tf_op jit(solution)/shard_map/all_gather | solution.py:136
  12.4 83.5 %collective-permute-start = (bf16[256,256]{1,0:T(8,128)(2,1)S(1)}, bf16[256,256]{1,0:T(8,128)(2,1)}, u32[]{:S(2)}, u32[]{:S(2)}) collective-permute-start(bf16[256,256]{1,0:T(8,128)(2,1)S(1)} %get-tuple-element.18), channel_id=1, source_target_pairs={{0,1},{1,2},{2,3},{3,4},{4,5},{5,6},{6,7},{7,8},{8,9},{9,10},{10,1... | collective-permute-start | bytes 393224 | tf_op jit(solution)/shard_map/ppermute | solution.py:20
  16.9 79.0 %collective-permute-start.1 = (bf16[256,256]{1,0:T(8,128)(2,1)S(1)}, bf16[256,256]{1,0:T(8,128)(2,1)}, u32[]{:S(2)}, u32[]{:S(2)}) collective-permute-start(bf16[256,256]{1,0:T(8,128)(2,1)S(1)} %get-tuple-element.17), channel_id=1, source_target_pairs={{1,0},{2,1},{3,2},{4,3},{5,4},{6,5},{7,6},{8,7},{9,8},{10,9},{11,1... | collective-permute-start | bytes 393224 | tf_op jit(solution)/shard_map/ppermute | solution.py:21
  18.9 364.0 %all-reduce.3.cloned.1.call-start = ((), (), s32[]{:S(2)}) async-start(), calls=%async_computation.2 | async-start | bytes 4194304 | tf_op jit(solution)/shard_map/psum | solution.py:164
  74.5 16.5 %copy-start.15 = (bf16[3,2048,256]{2,1,0:T(8,128)(2,1)S(1)}, bf16[3,2048,256]{2,1,0:T(8,128)(2,1)}, u32[]{:S(2)}) copy-start(bf16[3,2048,256]{2,1,0:T(8,128)(2,1)} %param.26) | copy-start | bytes 9437188
  92.1 5.9 copy-start.9
  92.1 292.3 %copy-start.7 = (bf16[1,2048,256]{2,1,0:T(8,128)(2,1)}, bf16[1,2048,256]{2,1,0:T(8,128)(2,1)S(1)}, u32[]{:S(2)}) copy-start(bf16[1,2048,256]{2,1,0:T(8,128)(2,1)S(1)} %get-tuple-element.8) | copy-start | bytes 3145732
  159.7 325.8 %all-gather.14.cloned.1.call-start = ((), (), s32[]{:S(2)}) async-start(), calls=%async_computation.5 | async-start | bytes 9437184 | tf_op jit(solution)/shard_map/all_gather | solution.py:161
  313.1 70.9 %copy-start.16 = (bf16[32,2048]{1,0:T(8,128)(2,1)S(1)}, bf16[32,2048]{1,0:T(8,128)(2,1)}, u32[]{:S(2)}) copy-start(bf16[32,2048]{1,0:T(8,128)(2,1)} %param.28) | copy-start | bytes 393220
  384.5 4.4 copy-start.12
  384.5 4.4 copy-start.20
  384.5 4.4 copy-start.21
  384.6 4.4 copy-start.22
  384.6 4.4 copy-start.23
  392.3 93.1 %copy-start.6 = (bf16[32,16384]{1,0:T(8,128)(2,1)S(1)}, bf16[32,16384]{1,0:T(8,128)(2,1)}, u32[]{:S(2)}) copy-start(bf16[32,16384]{1,0:T(8,128)(2,1)} %all-gather.6.cloned.1.call-done) | copy-start | bytes 3145732
  392.4 251.0 %all-reduce.5.cloned.1.call-start = ((), (), s32[]{:S(2)}) async-start(), calls=%async_computation.6 | async-start | bytes 4194304 | tf_op jit(solution)/shard_map/psum | solution.py:164
  501.2 8.8 %collective-permute-start.2 = (bf16[256,256]{1,0:T(8,128)(2,1)S(1)}, bf16[256,256]{1,0:T(8,128)(2,1)S(1)}, u32[]{:S(2)}, u32[]{:S(2)}) collective-permute-start(bf16[256,256]{1,0:T(8,128)(2,1)S(1)} %get-tuple-element.13), channel_id=1, source_target_pairs={{0,1},{1,2},{2,3},{3,4},{4,5},{5,6},{6,7},{7,8},{8,9},{9,10},{10,1... | collective-permute-start | bytes 393224 | tf_op jit(solution)/shard_map/ppermute | solution.py:20
  505.1 7.6 %collective-permute-start.3 = (bf16[256,256]{1,0:T(8,128)(2,1)S(1)}, bf16[256,256]{1,0:T(8,128)(2,1)S(1)}, u32[]{:S(2)}, u32[]{:S(2)}) collective-permute-start(bf16[256,256]{1,0:T(8,128)(2,1)S(1)} %get-tuple-element.14), channel_id=1, source_target_pairs={{1,0},{2,1},{3,2},{4,3},{5,4},{6,5},{7,6},{8,7},{9,8},{10,9},{11,1... | collective-permute-start | bytes 393224 | tf_op jit(solution)/shard_map/ppermute | solution.py:21
  515.5 129.3 %copy-start.8 = (bf16[1,2048,256]{2,1,0:T(8,128)(2,1)S(1)}, bf16[1,2048,256]{2,1,0:T(8,128)(2,1)}, u32[]{:S(2)}) copy-start(bf16[1,2048,256]{2,1,0:T(8,128)(2,1)} %copy-done.7) | copy-start | bytes 3145732
  644.9 4.7 copy-start.13
  (14 other events, 33.2 us)
Sparse Core Ops, SparseCore 0:
  9.6 36.9 all-gather.5
  48.8 95.9 all-gather.7
  147.3 44.1 all-gather.9
  193.8 43.5 all-gather.11
  240.3 142.5 all-reduce.2
  392.5 92.9 all-gather.13
  500.1 143.1 all-reduce.4
where the time goes:
time: 663 us; the launch traced here: 662 us
  waiting for transfers between devices  415 us (63%)
  local copies, waits for them, and re-layouts  122 us (18%)
  other arithmetic  51.6 us (8%)
  matrix products  47 us (7%)
  between operations  14.5 us (2%)
  starting transfers between devices  12.6 us (2%)
    psum x2, waiting for transfers between devices, stress(): lax.psum(partial_sum.astype(jnp.bfloat16), 'col').astype(jnp.float32)  195 us
    all_gather x2, waiting for transfers between devices, stress(): slip_all = lax.all_gather(rounded, 'row', axis=0, tiled=True)  138 us
    gather x1, local copies, waits for them, and re-layouts, fault_pressure(): joined[adj_bricks.reshape(slots * patches)]  66.4 us
    all_gather x1, waiting for transfers between devices, per_device(): lax.all_gather(pressure_rate, 'col', axis=0, tiled=True)  45.9 us
    unnamed x57, local copies, waits for them, and re-layouts  41.4 us
    all_gather x1, waiting for transfers between devices, per_device(): lax.all_gather(pressure_now, 'col', axis=0, tiled=True)  31.6 us
    select_n x1, other arithmetic, per_device(): masked = jnp.where(keep, matrix, jnp.zeros((), jnp.bfloat16))  22.4 us
    dot_general x2, matrix products, stress(): partial_sum = jnp.dot(masked, coeff, preferred_element_type=jnp.float32)  19.3 us
  transfers between devices with their start and end apart: 11, of which 7 were waited for; matrix products, arithmetic and copies ran while one was open for 28% of the time, Pallas kernels for 0%

commit v1 on v0

--- a/solution.py
+++ b/solution.py
@@ -8,6 +8,11 @@
 BPD = 8
 STEP_SIZE = 0.5
 REF_FRICTION = 0.6
+
+
+def add_all(array, mesh_axis):
+    parts = lax.all_gather(array, mesh_axis)
+    return jnp.sum(parts, axis=0)
 
 
 def with_halo(array, sides, width):
@@ -161,7 +166,7 @@
         slip_all = lax.all_gather(rounded, "row", axis=0, tiled=True)
         coeff = project(basis_all, slip_all)
         partial_sum = jnp.dot(masked, coeff, preferred_element_type=jnp.float32)
-        total = lax.psum(partial_sum.astype(jnp.bfloat16), "col").astype(jnp.float32)
+        total = add_all(partial_sum.astype(jnp.bfloat16), "col").astype(jnp.float32)
         mine = lax.dynamic_slice_in_dim(total, col_index * share, share, 0)
         far_coeff = mine.astype(jnp.bfloat16)
         far = jnp.einsum(

time: 663 us -> 770 us (1.16)
  waiting for transfers between devices: 415 us -> 499 us
  other arithmetic: 51.6 us -> 75.2 us
    all_gather x0 -> x2, waiting for transfers between devices: none -> 283 us  [add_all(): parts = lax.all_gather(array, mesh_axis)]
    psum x2 -> x0, waiting for transfers between devices: 195 us -> none  [stress(): lax.psum(partial_sum.astype(jnp.bfloat16), 'col').astype(jnp.float32)]
    reduce_sum x0 -> x2, other arithmetic: none -> 24.6 us  [add_all(): return jnp.sum(parts, axis=0)]
    all_gather x1, waiting for transfers between devices: 31.6 us -> 17 us  [per_device(): lax.all_gather(pressure_now, 'col', axis=0, tiled=True)]
    all_gather x2, waiting for transfers between devices: 138 us -> 150 us  [stress(): slip_all = lax.all_gather(rounded, 'row', axis=0, tiled=True)]
    unnamed x57 -> x59, local copies, waits for them, and re-layouts: 41.4 us -> 46.4 us
  transfers between devices with their start and end apart: 11 -> 11, of which waited for: 7 -> 7; matrix products, arithmetic and copies ran while one was open for 28% -> 23% of each run, Pallas kernels for 0% -> 0%
where the time goes in v1:
time: 770 us
  waiting for transfers between devices  499 us (65%)
  local copies, waits for them, and re-layouts  127 us (16%)
  other arithmetic  75.2 us (10%)
  matrix products  41.9 us (5%)
  between operations  14.5 us (2%)
  starting transfers between devices  12.2 us (2%)
    all_gather x2, waiting for transfers between devices, add_all(): parts = lax.all_gather(array, mesh_axis)  283 us
    all_gather x2, waiting for transfers between devices, stress(): slip_all = lax.all_gather(rounded, 'row', axis=0, tiled=True)  150 us
    gather x1, local copies, waits for them, and re-layouts, fault_pressure(): joined[adj_bricks.reshape(slots * patches)]  66.2 us
    unnamed x59, local copies, waits for them, and re-layouts  46.4 us
    all_gather x1, waiting for transfers between devices, per_device(): lax.all_gather(pressure_rate, 'col', axis=0, tiled=True)  45.9 us
    reduce_sum x2, other arithmetic, add_all(): return jnp.sum(parts, axis=0)  24.6 us
    select_n x1, other arithmetic, per_device(): masked = jnp.where(keep, matrix, jnp.zeros((), jnp.bfloat16))  22.4 us
    all_gather x1, waiting for transfers between devices, per_device(): lax.all_gather(pressure_now, 'col', axis=0, tiled=True)  17 us
  transfers between devices with their start and end apart: 11, of which 7 were waited for; matrix products, arithmetic and copies ran while one was open for 23% of the time, Pallas kernels for 0%

profile of v1, /device:TPU:1, one launch (start us, length us, event | category | flops | bytes accessed | tf_op | source)
XLA Modules:
  0.0 769.5 jit_solution(8574325838573936437)
XLA Ops:
  13.8 11.3 %broadcast_in_dim.14 = f32[128,32,2048]{2,1,0:T(8,128)} broadcast(f32[128,2048]{1,0:T(8,128)S(1)} %copy.23), dimensions={0,2} | broadcast | bytes 34603008 | tf_op jit(solution)/shard_map/broadcast_in_dim | solution.py:60
  25.1 19.9 %copy.30 = f32[512,8,8,256]{3,2,1,0:T(8,128)S(1)} copy(f32[512,8,8,256]{3,1,2,0:T(8,128)} %bitcast.101) | data formatting | bytes 67108864
  45.1 22.4 %fusion.2 = bf16[4096,8,256]{2,1,0:T(8,128)(2,1)} fusion(bf16[4096,8,256]{2,1,0:T(8,128)(2,1)} %param.29, f32[512,8,8,256]{3,2,1,0:T(8,128)S(1)} %copy.30, s32[8,256]{1,0:T(8,128)S(1)} %add_select_fusion.2, s32[4096]{0:T(1024)S(1)} %add_select_fusion, s32[8,256]{1,0:T(8,128)S(1)} %broadcast_in_dim.13, s32[4096]{0:T(1024)S(1)} %sub.77), kind=kLoop, calls=%fused_computation.6 | loop fusion | flops 67108864 | bytes 67158016 | tf_op jit(solution)/shard_map/jit(_where)/select_n | solution.py:160
  67.5 16.3 %copy.31 = bf16[512,8,8,256]{3,1,2,0:T(8,128)(2,1)} copy(bf16[512,8,8,256]{3,2,1,0:T(8,128)(2,1)} %bitcast.103) | data formatting | bytes 33554432
  83.9 61.0 %all-gather.12.cloned.1.call-done = bf16[16384,256]{1,0:T(8,128)(2,1)} async-done(((bf16[2048,256]{1,0:T(8,128)(2,1)}), bf16[16384,256]{1,0:T(8,128)(2,1)}) %all-gather.12.cloned.1.call-update) | async-done | bytes 8388624 | tf_op jit(solution)/shard_map/all_gather | solution.py:166
  144.8 5.3 convolution_convert_fusion.3
  150.1 3.2 copy-done.6
  153.3 5.7 convolution_convert_fusion.1
  160.2 3.8 collective-permute-start
  174.5 17.0 %all-gather.14.cloned.1.call-done = bf16[2048,256]{1,0:T(8,128)(2,1)} async-done(((bf16[128,256]{1,0:T(8,128)(2,1)}), bf16[2048,256]{1,0:T(8,128)(2,1)}) %all-gather.14.cloned.1.call-update) | async-done | bytes 1048592 | tf_op jit(solution)/shard_map/all_gather | solution.py:140
  191.5 45.9 %all-gather.16.cloned.1.call-done = bf16[2048,256]{1,0:T(8,128)(2,1)} async-done(((bf16[128,256]{1,0:T(8,128)(2,1)}), bf16[2048,256]{1,0:T(8,128)(2,1)}) %all-gather.16.cloned.1.call-update) | async-done | bytes 1048592 | tf_op jit(solution)/shard_map/all_gather | solution.py:141
  239.1 66.2 %gather_fusion = bf16[16384,512]{1,0:T(8,128)(2,1)} fusion(bf16[2048,512]{1,0:T(8,128)(2,1)S(1)} %pad_maximum_fusion, s32[16384]{0:T(1024)S(1)} %broadcast_clamp_fusion), kind=kCustom, calls=%fused_computation | custom fusion | bytes 33619968 | tf_op jit(solution)/shard_map/gather | solution.py:38
  305.3 7.5 fusion
  315.1 111.0 %all-gather.20.cloned.1.call-done = bf16[65536,256]{1,0:T(8,128)(2,1)} async-done(((bf16[4096,256]{1,0:T(8,128)(2,1)}), bf16[65536,256]{1,0:T(8,128)(2,1)}) %all-gather.20.cloned.1.call-update) | async-done | bytes 33554448 | tf_op jit(solution)/shard_map/all_gather | solution.py:14
  426.1 11.6 %reduce_sum.42 = bf16[4096,256]{1,0:T(8,128)(2,1)S(1)} reduce(bf16[16,4096,256]{2,1,0:T(8,128)(2,1)} %bitcast.104, bf16[]{:T(256)} %constant.71.clone.1), dimensions={0}, to_apply=%region_0.0 | reduce | flops 15728640 | bytes 35651584 | tf_op jit(solution)/shard_map/reduce_sum | solution.py:15
  443.8 3.4 fusion.15
  447.3 88.8 %all-gather.18.cloned.1.call-done = bf16[16384,256]{1,0:T(8,128)(2,1)} async-done(((bf16[2048,256]{1,0:T(8,128)(2,1)}), bf16[16384,256]{1,0:T(8,128)(2,1)}) %all-gather.18.cloned.1.call-update) | async-done | bytes 8388624 | tf_op jit(solution)/shard_map/all_gather | solution.py:166
  536.1 4.8 convolution_convert_fusion.2
  540.9 9.6 %convolution_convert_fusion = bf16[4096,256]{1,0:T(8,128)(2,1)} fusion(bf16[4096,2048]{1,0:T(8,128)(2,1)} %bitcast.110, bf16[2048,256]{1,0:T(8,128)(2,1)S(1)} %bitcast.124), kind=kOutput, calls=%fused_computation.7 | convolution fusion | flops 4296015872 | bytes 19922944 | tf_op jit(solution)/shard_map/dot_general | solution.py:168
  551.8 3.8 collective-permute-start.2
  557.8 3.1 fusion.47
  564.9 172.4 %all-gather.22.cloned.1.call-done = bf16[65536,256]{1,0:T(8,128)(2,1)} async-done(((bf16[4096,256]{1,0:T(8,128)(2,1)}), bf16[65536,256]{1,0:T(8,128)(2,1)}) %all-gather.22.cloned.1.call-update) | async-done | bytes 33554448 | tf_op jit(solution)/shard_map/all_gather | solution.py:14
  737.3 13.0 %reduce_sum.45 = bf16[4096,256]{1,0:T(8,128)(2,1)} reduce(bf16[16,4096,256]{2,1,0:T(8,128)(2,1)} %bitcast.105, bf16[]{:T(256)} %constant.71.clone.1), dimensions={0}, to_apply=%region_3.4 | reduce | flops 15728640 | bytes 35651584 | tf_op jit(solution)/shard_map/reduce_sum | solution.py:15
  756.6 4.3 multiply_add_fusion
  (111 shorter events, 43.6 us)
Async XLA Ops:
  7.2 76.7 %all-gather.10.cloned.1.call-start = ((), (), s32[]{:S(2)}) async-start(), calls=%async_computation | async-start | bytes 1179648 | tf_op jit(solution)/shard_map/all_gather | solution.py:162
  7.9 4.6 copy-start.25
  7.9 136.9 %all-gather.12.cloned.1.call-start = ((), (), s32[]{:S(2)}) async-start(), calls=%async_computation.1 | async-start | bytes 9437184 | tf_op jit(solution)/shard_map/all_gather | solution.py:166
  10.6 180.9 %all-gather.14.cloned.1.call-start = ((), (), s32[]{:S(2)}) async-start(), calls=%async_computation.2 | async-start | bytes 1114112 | tf_op jit(solution)/shard_map/all_gather | solution.py:140
  11.4 226.0 %all-gather.16.cloned.1.call-start = ((), (), s32[]{:S(2)}) async-start(), calls=%async_computation.3 | async-start | bytes 1114112 | tf_op jit(solution)/shard_map/all_gather | solution.py:141
  12.0 414.2 %all-gather.20.cloned.1.call-start = ((), (), s32[]{:S(2)}) async-start(), calls=%async_computation.5 | async-start | bytes 35651584 | tf_op jit(solution)/shard_map/all_gather | solution.py:14
  144.8 8.5 %copy-start.6 = (bf16[512,8,8,256]{3,1,2,0:T(8,128)(2,1)S(1)}, bf16[512,8,8,256]{3,1,2,0:T(8,128)(2,1)}, u32[]{:S(2)}) copy-start(bf16[512,8,8,256]{3,1,2,0:T(8,128)(2,1)} %copy.31) | copy-start | bytes 50331652
  159.0 7.2 copy-start.18
  159.0 377.1 %all-gather.18.cloned.1.call-start = ((), (), s32[]{:S(2)}) async-start(), calls=%async_computation.4 | async-start | bytes 9437184 | tf_op jit(solution)/shard_map/all_gather | solution.py:166
  160.2 10.4 %collective-permute-start = (bf16[256,256]{1,0:T(8,128)(2,1)S(1)}, bf16[256,256]{1,0:T(8,128)(2,1)}, u32[]{:S(2)}, u32[]{:S(2)}) collective-permute-start(bf16[256,256]{1,0:T(8,128)(2,1)S(1)} %get-tuple-element.18), channel_id=1, source_target_pairs={{0,1},{1,2},{2,3},{3,4},{4,5},{5,6},{6,7},{7,8},{8,9},{9,10},{10,1... | collective-permute-start | bytes 393224 | tf_op jit(solution)/shard_map/ppermute | solution.py:25
  164.0 6.6 collective-permute-start.1
  168.3 4.4 copy-start.10
  168.3 270.0 %copy-start.8 = (bf16[1,2048,256]{2,1,0:T(8,128)(2,1)}, bf16[1,2048,256]{2,1,0:T(8,128)(2,1)S(1)}, u32[]{:S(2)}) copy-start(bf16[1,2048,256]{2,1,0:T(8,128)(2,1)S(1)} %get-tuple-element.8) | copy-start | bytes 3145732
  426.1 11.7 %copy-start.17 = (bf16[32,2048]{1,0:T(8,128)(2,1)S(1)}, bf16[32,2048]{1,0:T(8,128)(2,1)}, u32[]{:S(2)}) copy-start(bf16[32,2048]{1,0:T(8,128)(2,1)} %param.28) | copy-start | bytes 393220
  439.4 4.4 copy-start.14
  439.4 4.4 copy-start.21
  439.4 4.4 copy-start.22
  439.4 4.4 copy-start.23
  439.4 4.4 copy-start.24
  447.2 88.9 %copy-start.7 = (bf16[32,16384]{1,0:T(8,128)(2,1)S(1)}, bf16[32,16384]{1,0:T(8,128)(2,1)}, u32[]{:S(2)}) copy-start(bf16[32,16384]{1,0:T(8,128)(2,1)} %all-gather.10.cloned.1.call-done) | copy-start | bytes 3145732
  447.2 290.1 %all-gather.22.cloned.1.call-start = ((), (), s32[]{:S(2)}) async-start(), calls=%async_computation.6 | async-start | bytes 35651584 | tf_op jit(solution)/shard_map/all_gather | solution.py:14
  551.8 9.0 %collective-permute-start.2 = (bf16[256,256]{1,0:T(8,128)(2,1)S(1)}, bf16[256,256]{1,0:T(8,128)(2,1)S(1)}, u32[]{:S(2)}, u32[]{:S(2)}) collective-permute-start(bf16[256,256]{1,0:T(8,128)(2,1)S(1)} %get-tuple-element.13), channel_id=1, source_target_pairs={{0,1},{1,2},{2,3},{3,4},{4,5},{5,6},{6,7},{7,8},{8,9},{9,10},{10,1... | collective-permute-start | bytes 393224 | tf_op jit(solution)/shard_map/ppermute | solution.py:25
  555.7 6.3 collective-permute-start.3
  751.9 4.7 copy-start.15
  (15 other events, 31.6 us)
Sparse Core Ops, SparseCore 0:
  9.6 36.8 all-gather.9
  48.8 95.9 all-gather.11
  147.3 44.2 all-gather.13
  193.8 43.5 all-gather.15
  240.3 185.8 all-gather.19
  447.4 88.6 all-gather.17
  550.7 186.5 all-gather.21
